TPU v7x, 32 devices: a whole 2x2x4 slice. The times are simulated.
32 devices in a mesh: mem: 8 (over z, y), job: 4 (over x, core).
Axes of the slice: x: 2, y: 2, z: 4, core: 2. Of those that a mesh axis runs over, the one named last changes fastest.
Arguments:
- pair_cost: bfloat16 [1536, 128, 128], P(('mem', 'job')), may hold values from -6 to 6
- pair_coef: bfloat16 [1536, 128, 128], P(('mem', 'job')), may hold values from 0.049804688 to 0.5
- slot_member: int32 [32, 48], P(('mem', 'job')), may hold values from 0 to 31, never falling along the last dimension, each value on 1 to 4 neighbouring positions
- slot_owner: int32 [32, 48, 1], P(('mem', 'job')), may hold values from 0 to 7; in each aligned block of 48 rows (0 to 47, 48 to 95, ..., all dimensions but the last counted through in order) at most 9 rows name the same one
- slot_local: int32 [32, 48], P(('mem', 'job')), may hold values from 0 to 15
- duals: float32 [512, 128], P(('mem', 'job')), may hold values from 0.1 to 3
- capacity: int32 [512, 128], P(('mem', 'job')), may hold values from 0 to 39
Outputs:
- primal: bfloat16 [1536, 128, 128], P(('mem', 'job'))
- gradient: float32 [512, 128], P(('mem', 'job'))
- member_share: float32 [256, 128], P('mem')
Inputs may be any that keep to these rules, and one draw needn't show every extreme that they name: `slot_member`: in each device's row the values never fall, every value appears, none more than 4 times, and one exactly 4 times. `slot_owner`: among the 48 entries of one device no value appears more than 9 times, and in some devices one appears exactly 9 times.
All inputs are finite; a program needn't handle non-finite values.
Results may differ from a plain program's by a relative error of at most 0.001.
Values sent between devices are 32-bit elements; how exact they have to be, the bound alone decides.
A program may use at most 64 MiB of HBM per device.

v0:
```python
import jax
import jax.numpy as jnp
from jax import lax
from jax.sharding import PartitionSpec as P

MB_DEV = 32
RIDGE = 1.0


def allocate(pair_cost, pair_coef, dual_rows):
    reduced = pair_cost.astype(jnp.float32) + pair_coef.astype(jnp.float32) * dual_rows[:, None, :]
    allocation = jnp.clip(-reduced / RIDGE, 0.0, 1.0)
    column_part = jnp.sum(pair_coef.astype(jnp.float32) * allocation, axis=1)
    row_part = jnp.sum(allocation, axis=2)
    return (allocation.astype(jnp.bfloat16), column_part, row_part)


def per_device(pair_cost, pair_coef, slot_member, slot_owner, slot_local, duals, capacity):
    slot_count = pair_cost.shape[0]
    block_size = pair_cost.shape[1]
    job_blocks = duals.shape[0]
    mem_count = lax.axis_size("mem")
    owner_index = slot_owner[0, :, 0]
    local_index = slot_local[0]
    peer_slots = max(2, (3 * slot_count + 2 * mem_count - 1) // (2 * mem_count))
    owner_table = (owner_index[:, None] == jnp.arange(mem_count, dtype=jnp.int32)[None, :]).astype(
        jnp.int32
    )
    slot_rank = jnp.sum((jnp.cumsum(owner_table, axis=0) - owner_table) * owner_table, axis=1)
    position = owner_index * peer_slots + slot_rank
    requests = jnp.zeros((mem_count * peer_slots,), jnp.int32).at[position].set(local_index)
    requests = requests.reshape(mem_count, peer_slots)
    received = lax.all_to_all(requests, "mem", split_axis=0, concat_axis=0, tiled=True)
    replies = duals[received]
    fetched, received = (
        lax.all_to_all(replies, "mem", split_axis=0, concat_axis=0, tiled=True),
        received,
    )
    dual_rows = fetched.reshape(mem_count * peer_slots, block_size)[position]
    primal, column_part, row_part = allocate(pair_cost, pair_coef, dual_rows)
    outgoing = (
        jnp.zeros((mem_count * peer_slots, block_size), jnp.float32).at[position].set(column_part)
    )
    incoming = lax.all_to_all(
        outgoing.reshape(mem_count, peer_slots, block_size),
        "mem",
        split_axis=0,
        concat_axis=0,
        tiled=True,
    )
    totals = jax.ops.segment_sum(
        incoming.reshape(mem_count * peer_slots, block_size),
        received.reshape(-1),
        num_segments=job_blocks,
    )
    gradient = totals - capacity.astype(jnp.float32)
    member_table = (jnp.arange(MB_DEV, dtype=jnp.int32)[:, None] == slot_member[0][None, :]).astype(
        jnp.float32
    )
    member_part = jnp.dot(
        member_table, row_part, precision=lax.Precision.HIGHEST, preferred_element_type=jnp.float32
    )
    member_share = lax.psum(member_part, "job") / block_size
    return (primal, gradient, member_share)


def solution(mesh):
    placed = (
        P(("mem", "job"), None, None),
        P(("mem", "job"), None, None),
        P(("mem", "job"), None),
        P(("mem", "job"), None, None),
        P(("mem", "job"), None),
        P(("mem", "job"), None),
        P(("mem", "job"), None),
    )
    return jax.shard_map(
        per_device,
        mesh=mesh,
        in_specs=placed,
        out_specs=(P(("mem", "job"), None, None), P(("mem", "job"), None), P("mem", None)),
        check_vma=False,
    )
```

profile of v0, /device:TPU:0, one launch (start us, length us, event | category | flops | bytes accessed | tf_op | source)
XLA Modules:
  0.0 57.0 jit_solution(11159333356886695551)
XLA Ops:
  0.6 0.0 copy-start
  0.6 0.7 %fusion.6 = s32[48,8]{1,0:T(8,128)S(1)} fusion(s32[48]{0:T(128)} %bitcast.20), kind=kLoop, calls=%fused_computation.15 | loop fusion | flops 768 | bytes 1728 | tf_op jit(solution)/shard_map/convert_element_type | solution.py:26
  1.4 0.1 reduce_window_sum.11
  1.5 0.8 %select_reduce_fusion = s32[48]{0:T(128)S(1)} fusion(s32[48,8]{1,0:T(8,128)S(1)} %reduce_window_sum.11, s32[48]{0:T(128)} %bitcast.21), kind=kLoop, calls=%fused_computation.13 | loop fusion | flops 1872 | bytes 1920 | tf_op jit(solution)/shard_map/reduce_sum | solution.py:29
  2.3 0.7 %fusion.13 = s32[48]{0:T(128)S(1)} fusion(s32[48]{0:T(128)S(1)} %select_reduce_fusion, s32[1,48,1]{1,2,0:T(1,128)} %param.10), kind=kLoop, calls=%fused_computation.29 | loop fusion | flops 240 | bytes 576 | tf_op jit(solution)/shard_map/select_n | solution.py:31
  3.0 0.9 %scatter_custom_fusion = s32[72]{0:T(128)S(1)} fusion(s32[48]{0:T(128)S(1)} %fusion.13, s32[48]{0:T(128)} %bitcast.23, s32[]{:T(128)} %constant.8.clone.1), kind=kCustom, calls=%fused_computation.31 | custom fusion | bytes 800 | tf_op jit(solution)/shard_map/scatter | solution.py:31
  3.8 0.1 all_to_all.14
  3.9 13.6 %all_to_all.22 = s32[8,1,9]{2,1,0:T(1,128)S(1)} all-to-all(s32[8,1,9]{2,1,0:T(1,128)S(1)} %bitcast.19), channel_id=1, replica_groups=mesh['mem'=8,'job'=4] {'mem'}, dimensions={0} | all-to-all | bytes 576 | tf_op jit(solution)/shard_map/all_to_all | solution.py:33
  17.5 0.1 reshape.83
  17.6 0.0 copy-done
  17.6 0.6 %gather_fusion = f32[72,128]{1,0:T(8,128)S(1)} fusion(f32[16,128]{1,0:T(8,128)S(1)} %copy-done, s32[1024]{0:T(1024)S(1)} %pad_clamp_fusion.1), kind=kCustom, calls=%fused_computation | custom fusion | bytes 74016 | tf_op jit(solution)/shard_map/gather | solution.py:34
  18.2 0.6 %reshape.82 = f32[8,9,128]{2,1,0:T(8,128)} reshape(f32[72,128]{1,0:T(8,128)S(1)} %gather_fusion) | data formatting | bytes 73728 | tf_op jit(solution)/shard_map/gather | solution.py:34
  18.8 3.4 %all-to-all-start.1 = ((f32[8,9,128]{2,1,0:T(8,128)}), f32[8,9,128]{2,1,0:T(8,128)S(1)}, u32[]{:S(2)}, u32[]{:S(2)}) async-start(f32[8,9,128]{2,1,0:T(8,128)} %reshape.82), calls=%async_computation.1 | async-start | bytes 131072 | tf_op jit(solution)/shard_map/all_to_all | solution.py:36
  22.2 0.5 broadcast.65
  22.7 0.7 %reduce.3 = s32[8,9]{1,0:T(8,128)S(1)} reduce(s32[8,1,9]{2,1,0:T(1,128)S(1)} %all_to_all.22, s32[]{:T(128)} %broadcast.65), dimensions={1}, to_apply=%all_to_all.15.reduce_sub_computation.3 | reduce | bytes 580 | tf_op jit(solution)/shard_map/all_to_all | solution.py:33
  23.4 0.1 reshape.115
  23.5 5.6 %all-to-all-done.1 = f32[8,9,128]{2,1,0:T(8,128)S(1)} async-done(((f32[8,9,128]{2,1,0:T(8,128)}), f32[8,9,128]{2,1,0:T(8,128)S(1)}, u32[]{:S(2)}, u32[]{:S(2)}) %all-to-all-start.1) | async-done | bytes 36896 | tf_op jit(solution)/shard_map/all_to_all | solution.py:36
  29.0 0.6 %gather_fusion.1 = f32[48,128]{1,0:T(8,128)S(1)} fusion(f32[72,128]{1,0:T(8,128)S(1)} %reshape.78, s32[1024]{0:T(1024)S(1)} %pad_clamp_fusion), kind=kCustom, calls=%fused_computation.1 | custom fusion | bytes 49344 | tf_op jit(solution)/shard_map/gather | solution.py:39
  29.6 0.0 copy-start.2
  29.6 0.0 copy-start.1
  29.6 4.1 %fusion.4 = (f32[48,128]{1,0:T(8,128)S(1)}, f32[48,128]{1,0:T(8,128)S(1)}, bf16[48,128,128]{2,1,0:T(8,128)(2,1)}) fusion(bf16[48,128,128]{2,1,0:T(8,128)(2,1)} %param.8, bf16[48,128,128]{2,1,0:T(8,128)(2,1)} %param.7, f32[48,128]{1,0:T(8,128)S(1)} %gather_fusion.1), kind=kLoop, calls=%fused_computation.11 | loop fusion | flops 7852032 | bytes 4792320 | tf_op jit(solution)/shard_map/reduce_sum | solution.py:14
  33.8 0.0 copy-done.2
  33.8 0.1 fusion.9
  33.9 10.1 %psum.7 = f32[32,128]{1,0:T(8,128)S(1)} all-reduce(f32[32,128]{1,0:T(8,128)S(1)} %fusion.9), channel_id=1, replica_groups=mesh['mem'=8,'job'=4] {'job'}, use_global_device_ids=true, to_apply=%region_7.8 | all-reduce | flops 4096 | bytes 32768 | tf_op jit(solution)/shard_map/psum | solution.py:63
  44.0 0.7 %scatter_custom_fusion.1 = f32[72,128]{1,0:T(8,128)S(1)} fusion(s32[48]{0:T(128)S(1)} %fusion.13, f32[48,128]{1,0:T(8,128)S(1)} %get-tuple-element.4, f32[]{:T(128)} %constant.7.clone.1), kind=kCustom, calls=%fused_computation.16 | custom fusion | bytes 36868 | tf_op jit(solution)/shard_map/scatter | solution.py:42
  44.7 0.6 %reshape.79 = f32[8,9,128]{2,1,0:T(8,128)} reshape(f32[72,128]{1,0:T(8,128)S(1)} %scatter_custom_fusion.1) | data formatting | bytes 73728 | tf_op jit(solution)/shard_map/reshape | solution.py:45
  45.3 3.3 %all-to-all-start.2 = ((f32[8,9,128]{2,1,0:T(8,128)}), f32[8,9,128]{2,1,0:T(8,128)S(1)}, u32[]{:S(2)}, u32[]{:S(2)}) async-start(f32[8,9,128]{2,1,0:T(8,128)} %reshape.79), calls=%async_computation.2 | async-start | bytes 131072 | tf_op jit(solution)/shard_map/all_to_all | solution.py:44
  48.7 0.6 %broadcast_multiply_fusion = f32[32,128]{1,0:T(8,128)} fusion(f32[32,128]{1,0:T(8,128)S(1)} %psum.7), kind=kLoop, calls=%fused_computation.21 | loop fusion | flops 4096 | bytes 32768 | tf_op jit(solution)/shard_map/div | solution.py:63
  49.3 6.2 %all-to-all-done.2 = f32[8,9,128]{2,1,0:T(8,128)S(1)} async-done(((f32[8,9,128]{2,1,0:T(8,128)}), f32[8,9,128]{2,1,0:T(8,128)S(1)}, u32[]{:S(2)}, u32[]{:S(2)}) %all-to-all-start.2) | async-done | bytes 36896 | tf_op jit(solution)/shard_map/all_to_all | solution.py:44
  55.5 0.8 %scatter_custom_fusion.2 = f32[16,128]{1,0:T(8,128)S(1)} fusion(s32[72]{0:T(128)S(1)} %reshape.115, f32[72,128]{1,0:T(8,128)S(1)} %reshape.117, f32[]{:T(128)} %constant.7.clone.1), kind=kCustom, calls=%fused_computation.26 | custom fusion | flops 9216 | bytes 8196 | tf_op jit(solution)/shard_map/scatter-add | solution.py:51
  56.3 0.0 copy-done.1
  56.3 0.6 %convert_subtract_fusion = f32[16,128]{1,0:T(8,128)} fusion(f32[16,128]{1,0:T(8,128)S(1)} %scatter_custom_fusion.2, s32[16,128]{1,0:T(8,128)S(1)} %copy-done.1), kind=kLoop, calls=%fused_computation.23 | loop fusion | flops 4096 | bytes 24576 | tf_op jit(solution)/shard_map/sub | solution.py:56
  (5 shorter events, 0.0 us)
Async XLA Ops:
  0.6 17.0 %copy-start = (f32[16,128]{1,0:T(8,128)S(1)}, f32[16,128]{1,0:T(8,128)}, u32[]{:S(2)}) copy-start(f32[16,128]{1,0:T(8,128)} %param.12) | copy-start | bytes 24580
  18.8 10.2 %all-to-all-start.1 = ((f32[8,9,128]{2,1,0:T(8,128)}), f32[8,9,128]{2,1,0:T(8,128)S(1)}, u32[]{:S(2)}, u32[]{:S(2)}) async-start(f32[8,9,128]{2,1,0:T(8,128)} %reshape.82), calls=%async_computation.1 | async-start | bytes 131072 | tf_op jit(solution)/shard_map/all_to_all | solution.py:36
  29.6 4.1 %copy-start.2 = (s32[1,48]{1,0:T(1,128)S(1)}, s32[1,48]{1,0:T(1,128)}, u32[]{:S(2)}) copy-start(s32[1,48]{1,0:T(1,128)} %param.9) | copy-start | bytes 580
  29.6 26.7 %copy-start.1 = (s32[16,128]{1,0:T(8,128)S(1)}, s32[16,128]{1,0:T(8,128)}, u32[]{:S(2)}) copy-start(s32[16,128]{1,0:T(8,128)} %param.13) | copy-start | bytes 24580
  45.3 10.2 %all-to-all-start.2 = ((f32[8,9,128]{2,1,0:T(8,128)}), f32[8,9,128]{2,1,0:T(8,128)S(1)}, u32[]{:S(2)}, u32[]{:S(2)}) async-start(f32[8,9,128]{2,1,0:T(8,128)} %reshape.79), calls=%async_computation.2 | async-start | bytes 131072 | tf_op jit(solution)/shard_map/all_to_all | solution.py:44
where the time goes:
time: 57.4 us; the launch traced here: 57 us
  blocking collectives  23.7 us (41%)
  waiting for transfers between devices  11.8 us (21%)
  other arithmetic  9.12 us (16%)
  starting transfers between devices  6.7 us (12%)
  local copies, waits for them, and re-layouts  4.76 us (8%)
  between operations  0.73 us (1%)
    all_to_all x1, blocking collectives, per_device(): lax.all_to_all(requests, 'mem', split_axis=0, concat_axis=0, tiled=True)  13.6 us
    psum x1, blocking collectives, per_device(): member_share = lax.psum(member_part, 'job') / block_size  10.1 us
    all_to_all x1, waiting for transfers between devices, per_device(): lax.all_to_all(outgoing.reshape(mem_count, peer_slots, block_size), 'mem'...  6.23 us
    all_to_all x1, waiting for transfers between devices, per_device(): lax.all_to_all(replies, 'mem', split_axis=0, concat_axis=0, tiled=True)  5.57 us
    reduce_sum x1, other arithmetic, allocate(): row_part = jnp.sum(allocation, axis=2)  4.11 us
    all_to_all x1, starting transfers between devices, per_device(): lax.all_to_all(replies, 'mem', split_axis=0, concat_axis=0, tiled=True)  3.35 us
    all_to_all x1, starting transfers between devices, per_device(): lax.all_to_all(outgoing.reshape(mem_count, peer_slots, block_size), 'mem'...  3.35 us
    gather x2, local copies, waits for them, and re-layouts, per_device(): replies = duals[received]  1.24 us
  transfers between devices with their start and end apart: 2, of which 2 were waited for; matrix products, arithmetic and copies ran while one was open for 3% of the time, Pallas kernels for 0%

commit v1 on v0

--- a/solution.py
+++ b/solution.py
@@ -5,6 +5,30 @@
 
 MB_DEV = 32
 RIDGE = 1.0
+
+
+def in_blocks(array, dim, size):
+    shape = array.shape
+    pieces = array.reshape(*shape[:dim], size, shape[dim] // size, *shape[dim + 1 :])
+    return jnp.moveaxis(pieces, dim, 0)
+
+
+def laid_out(parts, dim):
+    shape = list(parts.shape[1:])
+    shape[dim] *= parts.shape[0]
+    return jnp.moveaxis(parts, 0, dim).reshape(shape)
+
+
+def rotated_exchange(shard, axis, split_dim, concat_dim):
+    length, here = (lax.axis_size(axis), lax.axis_index(axis))
+    pieces = in_blocks(shard, split_dim, length)
+    out = pieces
+    for step in range(1, length):
+        target, source = ((here + step) % length, (here - step) % length)
+        sent = lax.dynamic_index_in_dim(pieces, target, 0)
+        partner_block = lax.ppermute(sent, axis, [(i, (i + step) % length) for i in range(length)])
+        out = lax.dynamic_update_slice_in_dim(out, partner_block, source, axis=0)
+    return laid_out(out, concat_dim)
 
 
 def allocate(pair_cost, pair_coef, dual_rows):
@@ -32,10 +56,7 @@
     requests = requests.reshape(mem_count, peer_slots)
     received = lax.all_to_all(requests, "mem", split_axis=0, concat_axis=0, tiled=True)
     replies = duals[received]
-    fetched, received = (
-        lax.all_to_all(replies, "mem", split_axis=0, concat_axis=0, tiled=True),
-        received,
-    )
+    fetched, received = (rotated_exchange(replies, "mem", 0, 0), received)
     dual_rows = fetched.reshape(mem_count * peer_slots, block_size)[position]
     primal, column_part, row_part = allocate(pair_cost, pair_coef, dual_rows)
     outgoing = (

time: 57.4 us -> 65.7 us (1.14)
  blocking collectives: 23.7 us -> 10.1 us
  starting transfers between devices: 6.7 us -> 19.9 us
  waiting for transfers between devices: 11.8 us -> 20.8 us
    all_to_all x1 -> x0, blocking collectives: 13.6 us -> none  [per_device(): lax.all_to_all(requests, 'mem', split_axis=0, concat_axis=0, tiled=True)]
    ppermute x0 -> x7, starting transfers between devices: none -> 8.58 us  [rotated_exchange(): lax.ppermute(sent, axis, [(i, (i + step) % length) for i in range(length)])]
    ppermute x0 -> x7, waiting for transfers between devices: none -> 8.19 us  [rotated_exchange(): lax.ppermute(sent, axis, [(i, (i + step) % length) for i in range(length)])]
    all_to_all x1, starting transfers between devices: 3.35 us -> 7.31 us  [per_device(): lax.all_to_all(requests, 'mem', split_axis=0, concat_axis=0, tiled=True)]
    all_to_all x1, waiting for transfers between devices: 5.57 us -> 6.36 us  [per_device(): lax.all_to_all(requests, 'mem', split_axis=0, concat_axis=0, tiled=True)]
  transfers between devices with their start and end apart: 2 -> 9, of which waited for: 2 -> 4; matrix products, arithmetic and copies ran while one was open for 3% -> 3% of each run, Pallas kernels for 0% -> 0%
where the time goes in v1:
time: 65.7 us; the launch traced here: 65.3 us
  waiting for transfers between devices  20.8 us (32%)
  starting transfers between devices  19.9 us (30%)
  blocking collectives  10.1 us (15%)
  other arithmetic  8.76 us (13%)
  local copies, waits for them, and re-layouts  4.79 us (7%)
  between operations  0.82 us (1%)
    psum x1, blocking collectives, per_device(): member_share = lax.psum(member_part, 'job') / block_size  10.1 us
    ppermute x7, starting transfers between devices, rotated_exchange(): lax.ppermute(sent, axis, [(i, (i + step) % length) for i in range(length)])  8.58 us
    ppermute x7, waiting for transfers between devices, rotated_exchange(): lax.ppermute(sent, axis, [(i, (i + step) % length) for i in range(length)])  8.19 us
    all_to_all x1, starting transfers between devices, per_device(): lax.all_to_all(requests, 'mem', split_axis=0, concat_axis=0, tiled=True)  7.31 us
    all_to_all x1, waiting for transfers between devices, per_device(): lax.all_to_all(requests, 'mem', split_axis=0, concat_axis=0, tiled=True)  6.36 us
    all_to_all x1, waiting for transfers between devices, per_device(): lax.all_to_all(outgoing.reshape(mem_count, peer_slots, block_size), 'mem'...  6.3 us
    all_to_all x1, starting transfers between devices, per_device(): lax.all_to_all(outgoing.reshape(mem_count, peer_slots, block_size), 'mem'...  3.98 us
    reduce_sum x1, other arithmetic, allocate(): row_part = jnp.sum(allocation, axis=2)  3.63 us
  transfers between devices with their start and end apart: 9, of which 4 were waited for; matrix products, arithmetic and copies ran while one was open for 3% of the time, Pallas kernels for 0%

profile of v1, /device:TPU:0, one launch (start us, length us, event | category | flops | bytes accessed | tf_op | source)
XLA Modules:
  0.0 65.3 jit_solution(16654476113410152033)
XLA Ops:
  0.7 0.8 %fusion.6 = s32[48,8]{1,0:T(8,128)S(1)} fusion(s32[48]{0:T(128)} %bitcast.35), kind=kLoop, calls=%fused_computation.15 | loop fusion | flops 768 | bytes 1728 | tf_op jit(solution)/shard_map/convert_element_type | solution.py:50
  1.5 0.1 reduce_window_sum.11
  1.6 0.8 %select_reduce_fusion = s32[48]{0:T(128)S(1)} fusion(s32[48,8]{1,0:T(8,128)S(1)} %reduce_window_sum.11, s32[48]{0:T(128)} %bitcast.36), kind=kLoop, calls=%fused_computation.13 | loop fusion | flops 1872 | bytes 1920 | tf_op jit(solution)/shard_map/reduce_sum | solution.py:53
  2.4 0.7 %fusion.13 = s32[48]{0:T(128)S(1)} fusion(s32[48]{0:T(128)S(1)} %select_reduce_fusion, s32[1,48,1]{1,2,0:T(1,128)} %param.10), kind=kLoop, calls=%fused_computation.43 | loop fusion | flops 240 | bytes 576 | tf_op jit(solution)/shard_map/select_n | solution.py:55
  3.1 0.9 %scatter_custom_fusion = s32[72]{0:T(128)S(1)} fusion(s32[48]{0:T(128)S(1)} %fusion.13, s32[48]{0:T(128)} %bitcast.38, s32[]{:T(128)} %constant.115.clone.1), kind=kCustom, calls=%fused_computation.45 | custom fusion | bytes 800 | tf_op jit(solution)/shard_map/scatter | solution.py:55
  3.9 0.7 %all_to_all.11 = s32[8,1,9]{2,0,1:T(8,128)} reshape(s32[72]{0:T(128)S(1)} %scatter_custom_fusion) | data formatting | bytes 576 | tf_op jit(solution)/shard_map/all_to_all | solution.py:57
  4.6 7.3 %all-to-all-start = ((s32[8,1,9]{2,1,0:T(1,128)}), s32[8,1,9]{2,1,0:T(1,128)S(1)}, u32[]{:S(2)}, u32[]{:S(2)}) async-start(s32[8,1,9]{2,1,0:T(1,128)} %bitcast.5), calls=%async_computation | async-start | bytes 8192 | tf_op jit(solution)/shard_map/all_to_all | solution.py:57
  12.0 6.4 %all-to-all-done = s32[8,1,9]{2,1,0:T(1,128)S(1)} async-done(((s32[8,1,9]{2,1,0:T(1,128)}), s32[8,1,9]{2,1,0:T(1,128)S(1)}, u32[]{:S(2)}, u32[]{:S(2)}) %all-to-all-start) | async-done | bytes 320 | tf_op jit(solution)/shard_map/all_to_all | solution.py:57
  18.4 0.1 reshape.90
  18.4 0.6 gather_fusion
  19.1 0.6 collective-permute-start
  19.7 0.5 broadcast.79
  20.2 0.7 %reduce.3 = s32[8,9]{1,0:T(8,128)S(1)} reduce(s32[8,1,9]{2,1,0:T(1,128)S(1)} %all-to-all-done, s32[]{:T(128)} %broadcast.79), dimensions={1}, to_apply=%all_to_all.12.reduce_sub_computation.3 | reduce | bytes 580 | tf_op jit(solution)/shard_map/all_to_all | solution.py:57
  20.9 0.1 reshape.122
  21.0 4.2 %collective-permute-start.6 = (f32[1,1,9,128]{3,2,0,1:T(8,128)S(1)}, f32[1,1,9,128]{3,2,0,1:T(8,128)S(1)}, u32[]{:S(2)}, u32[]{:S(2)}) collective-permute-start(f32[1,1,9,128]{3,2,0,1:T(8,128)S(1)} %get-tuple-element.6), channel_id=1, source_target_pairs={{0,28},{4,0},{8,4},{12,8},{16,12},{20,16},{24,20},{28,24},{1,29},{... | collective-permute-start | bytes 13832 | tf_op jit(solution)/shard_map/ppermute | solution.py:29
  25.1 0.2 collective-permute-start.3
  25.4 2.7 %collective-permute-start.2 = (f32[1,1,9,128]{3,2,0,1:T(8,128)S(1)}, f32[1,1,9,128]{3,2,0,1:T(8,128)S(1)}, u32[]{:S(2)}, u32[]{:S(2)}) collective-permute-start(f32[1,1,9,128]{3,2,0,1:T(8,128)S(1)} %get-tuple-element.9), channel_id=1, source_target_pairs={{0,12},{4,16},{8,20},{12,24},{16,28},{20,0},{24,4},{28,8},{1,13},{... | collective-permute-start | bytes 13832 | tf_op jit(solution)/shard_map/ppermute | solution.py:29
  28.1 0.2 collective-permute-start.1
  28.3 5.2 %collective-permute-done.1 = f32[1,1,9,128]{3,2,0,1:T(8,128)S(1)} collective-permute-done((f32[1,1,9,128]{3,2,0,1:T(8,128)S(1)}, f32[1,1,9,128]{3,2,0,1:T(8,128)S(1)}, u32[]{:S(2)}, u32[]{:S(2)}) %collective-permute-start.1) | collective-permute-done | bytes 4640 | tf_op jit(solution)/shard_map/ppermute | solution.py:29
  33.5 0.6 collective-permute-start.5
  34.2 3.0 %collective-permute-done.5 = f32[1,1,9,128]{3,2,0,1:T(8,128)S(1)} collective-permute-done((f32[1,1,9,128]{3,2,0,1:T(8,128)S(1)}, f32[1,1,9,128]{3,2,0,1:T(8,128)S(1)}, u32[]{:S(2)}, u32[]{:S(2)}) %collective-permute-start.5) | collective-permute-done | bytes 4640 | tf_op jit(solution)/shard_map/ppermute | solution.py:29
  37.2 0.6 gather_fusion.1
  37.8 3.6 %fusion.4 = (f32[48,128]{1,0:T(8,128)S(1)}, f32[48,128]{1,0:T(8,128)S(1)}, bf16[48,128,128]{2,1,0:T(8,128)(2,1)}) fusion(bf16[48,128,128]{2,1,0:T(8,128)(2,1)S(1)} %copy-done.1, bf16[48,128,128]{2,1,0:T(8,128)(2,1)} %param.7, f32[48,128]{1,0:T(8,128)S(1)} %gather_fusion.1), kind=kLoop, calls=%fused_computation.11 | loop fusion | flops 7852032 | bytes 4792320 | tf_op jit(solution)/shard_map/reduce_sum | solution.py:38
  41.4 0.1 fusion.9
  41.6 10.1 %psum.7 = f32[32,128]{1,0:T(8,128)S(1)} all-reduce(f32[32,128]{1,0:T(8,128)S(1)} %fusion.9), channel_id=1, replica_groups=mesh['mem'=8,'job'=4] {'job'}, use_global_device_ids=true, to_apply=%region_7.8 | all-reduce | flops 4096 | bytes 32768 | tf_op jit(solution)/shard_map/psum | solution.py:84
  51.7 0.7 %scatter_custom_fusion.1 = f32[72,128]{1,0:T(8,128)S(1)} fusion(s32[48]{0:T(128)S(1)} %fusion.13, f32[48,128]{1,0:T(8,128)S(1)} %get-tuple-element.4, f32[]{:T(128)} %constant.114.clone.1), kind=kCustom, calls=%fused_computation.16 | custom fusion | bytes 36868 | tf_op jit(solution)/shard_map/scatter | solution.py:63
  52.4 0.6 reshape.86
  53.0 4.0 %all-to-all-start.1 = ((f32[8,9,128]{2,1,0:T(8,128)}), f32[8,9,128]{2,1,0:T(8,128)S(1)}, u32[]{:S(2)}, u32[]{:S(2)}) async-start(f32[8,9,128]{2,1,0:T(8,128)} %reshape.86), calls=%async_computation.1 | async-start | bytes 131072 | tf_op jit(solution)/shard_map/all_to_all | solution.py:65
  57.0 0.6 broadcast_multiply_fusion
  57.6 6.3 %all-to-all-done.1 = f32[8,9,128]{2,1,0:T(8,128)S(1)} async-done(((f32[8,9,128]{2,1,0:T(8,128)}), f32[8,9,128]{2,1,0:T(8,128)S(1)}, u32[]{:S(2)}, u32[]{:S(2)}) %all-to-all-start.1) | async-done | bytes 36896 | tf_op jit(solution)/shard_map/all_to_all | solution.py:65
  63.9 0.8 %scatter_custom_fusion.2 = f32[16,128]{1,0:T(8,128)S(1)} fusion(s32[72]{0:T(128)S(1)} %reshape.122, f32[72,128]{1,0:T(8,128)S(1)} %reshape.124, f32[]{:T(128)} %constant.114.clone.1), kind=kCustom, calls=%fused_computation.33 | custom fusion | flops 9216 | bytes 8196 | tf_op jit(solution)/shard_map/scatter-add | solution.py:72
  64.7 0.6 convert_subtract_fusion
  (29 shorter events, 0.1 us)
Async XLA Ops:
  0.6 17.8 %copy-start = (f32[16,128]{1,0:T(8,128)S(1)}, f32[16,128]{1,0:T(8,128)}, u32[]{:S(2)}) copy-start(f32[16,128]{1,0:T(8,128)} %param.12) | copy-start | bytes 24580
  0.6 37.1 %copy-start.1 = (bf16[48,128,128]{2,1,0:T(8,128)(2,1)S(1)}, bf16[48,128,128]{2,1,0:T(8,128)(2,1)}, u32[]{:S(2)}) copy-start(bf16[48,128,128]{2,1,0:T(8,128)(2,1)} %param.8) | copy-start | bytes 4718596
  4.6 13.7 %all-to-all-start = ((s32[8,1,9]{2,1,0:T(1,128)}), s32[8,1,9]{2,1,0:T(1,128)S(1)}, u32[]{:S(2)}, u32[]{:S(2)}) async-start(s32[8,1,9]{2,1,0:T(1,128)} %bitcast.5), calls=%async_computation | async-start | bytes 8192 | tf_op jit(solution)/shard_map/all_to_all | solution.py:57
  19.1 9.0 %collective-permute-start = (f32[1,1,9,128]{3,2,0,1:T(8,128)S(1)}, f32[1,1,9,128]{3,2,0,1:T(8,128)S(1)}, u32[]{:S(2)}, u32[]{:S(2)}) collective-permute-start(f32[1,1,9,128]{3,2,0,1:T(8,128)S(1)} %get-tuple-element.11), channel_id=1, source_target_pairs={{0,4},{4,8},{8,12},{12,16},{16,20},{20,24},{24,28},{28,0},{1,5},{5... | collective-permute-start | bytes 13832 | tf_op jit(solution)/shard_map/ppermute | solution.py:29
  21.0 16.2 %collective-permute-start.6 = (f32[1,1,9,128]{3,2,0,1:T(8,128)S(1)}, f32[1,1,9,128]{3,2,0,1:T(8,128)S(1)}, u32[]{:S(2)}, u32[]{:S(2)}) collective-permute-start(f32[1,1,9,128]{3,2,0,1:T(8,128)S(1)} %get-tuple-element.6), channel_id=1, source_target_pairs={{0,28},{4,0},{8,4},{12,8},{16,12},{20,16},{24,20},{28,24},{1,29},{... | collective-permute-start | bytes 13832 | tf_op jit(solution)/shard_map/ppermute | solution.py:29
  25.1 9.1 %collective-permute-start.4 = (f32[1,1,9,128]{3,2,0,1:T(8,128)S(1)}, f32[1,1,9,128]{3,2,0,1:T(8,128)S(1)}, u32[]{:S(2)}, u32[]{:S(2)}) collective-permute-start(f32[1,1,9,128]{3,2,0,1:T(8,128)S(1)} %get-tuple-element.7), channel_id=1, source_target_pairs={{0,20},{4,24},{8,28},{12,0},{16,4},{20,8},{24,12},{28,16},{1,21},{... | collective-permute-start | bytes 13832 | tf_op jit(solution)/shard_map/ppermute | solution.py:29
  25.1 9.0 %collective-permute-start.3 = (f32[1,1,9,128]{3,2,0,1:T(8,128)S(1)}, f32[1,1,9,128]{3,2,0,1:T(8,128)S(1)}, u32[]{:S(2)}, u32[]{:S(2)}) collective-permute-start(f32[1,1,9,128]{3,2,0,1:T(8,128)S(1)} %get-tuple-element.8), channel_id=1, source_target_pairs={{0,16},{4,20},{8,24},{12,28},{16,0},{20,4},{24,8},{28,12},{1,17},{... | collective-permute-start | bytes 13832 | tf_op jit(solution)/shard_map/ppermute | solution.py:29
  25.4 8.8 %collective-permute-start.2 = (f32[1,1,9,128]{3,2,0,1:T(8,128)S(1)}, f32[1,1,9,128]{3,2,0,1:T(8,128)S(1)}, u32[]{:S(2)}, u32[]{:S(2)}) collective-permute-start(f32[1,1,9,128]{3,2,0,1:T(8,128)S(1)} %get-tuple-element.9), channel_id=1, source_target_pairs={{0,12},{4,16},{8,20},{12,24},{16,28},{20,0},{24,4},{28,8},{1,13},{... | collective-permute-start | bytes 13832 | tf_op jit(solution)/shard_map/ppermute | solution.py:29
  28.1 5.4 %collective-permute-start.1 = (f32[1,1,9,128]{3,2,0,1:T(8,128)S(1)}, f32[1,1,9,128]{3,2,0,1:T(8,128)S(1)}, u32[]{:S(2)}, u32[]{:S(2)}) collective-permute-start(f32[1,1,9,128]{3,2,0,1:T(8,128)S(1)} %get-tuple-element.10), channel_id=1, source_target_pairs={{0,8},{4,12},{8,16},{12,20},{16,24},{20,28},{24,0},{28,4},{1,9},{5... | collective-permute-start | bytes 13832 | tf_op jit(solution)/shard_map/ppermute | solution.py:29
  33.5 3.7 %collective-permute-start.5 = (f32[1,1,9,128]{3,2,0,1:T(8,128)S(1)}, f32[1,1,9,128]{3,2,0,1:T(8,128)S(1)}, u32[]{:S(2)}, u32[]{:S(2)}) collective-permute-start(f32[1,1,9,128]{3,2,0,1:T(8,128)S(1)} %get-tuple-element.12), channel_id=1, source_target_pairs={{0,24},{4,28},{8,0},{12,4},{16,8},{20,12},{24,16},{28,20},{1,25},{... | collective-permute-start | bytes 13832 | tf_op jit(solution)/shard_map/ppermute | solution.py:29
  37.8 3.7 %copy-start.3 = (s32[1,48]{1,0:T(1,128)S(1)}, s32[1,48]{1,0:T(1,128)}, u32[]{:S(2)}) copy-start(s32[1,48]{1,0:T(1,128)} %param.9) | copy-start | bytes 580
  37.8 26.9 %copy-start.2 = (s32[16,128]{1,0:T(8,128)S(1)}, s32[16,128]{1,0:T(8,128)}, u32[]{:S(2)}) copy-start(s32[16,128]{1,0:T(8,128)} %param.13) | copy-start | bytes 24580
  53.0 10.9 %all-to-all-start.1 = ((f32[8,9,128]{2,1,0:T(8,128)}), f32[8,9,128]{2,1,0:T(8,128)S(1)}, u32[]{:S(2)}, u32[]{:S(2)}) async-start(f32[8,9,128]{2,1,0:T(8,128)} %reshape.86), calls=%async_computation.1 | async-start | bytes 131072 | tf_op jit(solution)/shard_map/all_to_all | solution.py:65
